TPU v7x, 128 devices: a whole 4x4x4 slice. The times are simulated.
128 devices in a mesh: lat: 16 (over z, x_lo, core), vec: 8 (over x_hi, y).
Axes of the slice: x: 4 (x_hi: 2, x_lo: 2; x = x_hi * 2 + x_lo), y: 4, z: 4, core: 2. Of those that a mesh axis runs over, the one named last changes fastest.
Arguments:
- vectors: bfloat16 [4, 128, 256, 1024], P(None, 'vec', 'lat'), may hold values from -6 to 6
- classical_spins: float32 [3, 256, 1024], P(None, 'lat'), may hold values from -1 to 1, as said below
- coefficients: float32 [5], replicated, may hold values from 0.4 to 1.6
Outputs:
- rotated_spins: float32 [3, 256, 1024], P(None, 'lat')
- local_fields: float32 [3, 256, 1024], P(None, 'lat')
Inputs may be any that keep to these rules, and one draw needn't show every extreme that they name: `classical_spins`: each site's spin has unit length.
All inputs are finite; a program needn't handle non-finite values.
Results may differ from a plain program's by a relative error of at most 0.0003.
Values sent between devices are 32-bit elements; how exact they have to be, the bound alone decides.
A program may use at most 64 MiB of HBM per device.

v0:
```python
import jax
import jax.numpy as jnp
from jax import lax
from jax.sharding import PartitionSpec as P

STEPS = 4
coupling = 2.0
hopping = 1.0
inverse_bound = 1.0 / 6.5
time_step = 1.0


def with_halo(block, sides, width):
    for axis, dim in sides:
        count = lax.axis_size(axis)
        forward = [(i, i + 1) for i in range(count - 1)]
        forward.append((count - 1, 0))
        backward = [(target, source) for source, target in forward]
        low = lax.ppermute(
            lax.slice_in_dim(block, block.shape[dim] - width, None, axis=dim), axis, forward
        )
        high = lax.ppermute(lax.slice_in_dim(block, 0, width, axis=dim), axis, backward)
        block = jnp.concatenate([low, block, high], axis=dim)
    return block


def exchange_term(states, spins_here):
    spin_x = spins_here[0][None]
    spin_y = spins_here[1][None]
    spin_z = spins_here[2][None]
    up_real, up_imag, down_real, down_imag = (states[0], states[1], states[2], states[3])
    return jnp.stack(
        [
            spin_z * up_real + spin_x * down_real + spin_y * down_imag,
            spin_z * up_imag + spin_x * down_imag - spin_y * down_real,
            spin_x * up_real - spin_y * up_imag - spin_z * down_real,
            spin_x * up_imag + spin_y * up_real - spin_z * down_imag,
        ]
    )


def spin_density(probes, weighted):
    along_x = jnp.sum(
        probes[0] * weighted[2]
        + probes[1] * weighted[3]
        + probes[2] * weighted[0]
        + probes[3] * weighted[1],
        axis=0,
    )
    along_y = jnp.sum(
        probes[0] * weighted[3]
        - probes[1] * weighted[2]
        - probes[2] * weighted[1]
        + probes[3] * weighted[0],
        axis=0,
    )
    along_z = jnp.sum(
        probes[0] * weighted[0]
        + probes[1] * weighted[1]
        - probes[2] * weighted[2]
        - probes[3] * weighted[3],
        axis=0,
    )
    return jnp.stack([along_x, along_y, along_z])


def rotate_spins(spins_now, fields):
    magnitude = jnp.sqrt(jnp.sum(fields * fields, axis=0))
    rotation_angle = time_step * magnitude
    cosine = jnp.cos(rotation_angle)
    sine_ratio = jnp.sinc(rotation_angle / jnp.pi)
    half_ratio = 0.5 * jnp.sinc(rotation_angle / (2.0 * jnp.pi)) ** 2
    torque = jnp.cross(fields, spins_now, axis=0)
    projection = jnp.sum(fields * spins_now, axis=0)
    return (
        cosine * spins_now
        + time_step * sine_ratio * torque
        + time_step * time_step * half_ratio * projection * fields
    )


def apply_hamiltonian(padded, spins_here):
    middle = padded[:, :, 1:-1]
    neighbours = (
        padded[:, :, 2:] + padded[:, :, :-2] + jnp.roll(middle, 1, 3) + jnp.roll(middle, -1, 3)
    )
    return inverse_bound * (coupling * exchange_term(middle, spins_here) - hopping * neighbours)


def shards(vectors, classical_spins, coefficients):
    probes = vectors.astype(jnp.float32)
    count_all = vectors.shape[1] * lax.axis_size("vec")
    moments = coefficients[0] * probes
    previous = probes
    current = probes
    for degree in range(STEPS):
        padded = with_halo(current, (("lat", 2),), 1)
        following = apply_hamiltonian(padded, classical_spins)
        if degree > 0:
            following = 2.0 * following - previous
        moments = moments + coefficients[degree + 1] * following
        previous = current
        current = following
    partial_value = spin_density(probes, moments) * (coupling / count_all)
    fields = lax.psum(partial_value, "vec")
    rotated = rotate_spins(classical_spins, fields)
    return (rotated, fields)


def solution(mesh):
    placed = (P(None, "vec", "lat", None), P(None, "lat", None), P())
    return jax.shard_map(
        shards,
        mesh=mesh,
        in_specs=placed,
        out_specs=(P(None, "lat", None), P(None, "lat", None)),
        check_vma=False,
    )
```

profile of v0, /device:TPU:0, one launch (start us, length us, event | category | flops | bytes accessed | tf_op | source)
XLA Modules:
  0.0 194.6 jit_solution(3503848978186060714)
XLA Ops:
  7.2 0.0 all-reduce.2.cloned.1.call-start
  7.2 2.8 %copy_convert_fusion = f32[4,16,16,1024]{3,1,2,0:T(8,128)S(1)} fusion(bf16[4,16,16,1024]{3,2,1,0:T(8,128)(2,1)} %param.4), kind=kLoop, calls=%fused_computation.36 | loop fusion | flops 1048576 | bytes 6291456 | tf_op jit(solution)/shard_map/convert_element_type | solution.py:91
  10.1 0.1 collective-permute-start.1
  10.2 0.0 copy-start.2
  10.2 0.0 copy-start.3
  10.2 4.6 %collective-permute-start = (f32[4,16,1,1024]{3,1,2,0:T(8,128)S(1)}, f32[4,16,1,1024]{3,1,2,0:T(8,128)S(1)}, u32[]{:S(2)}, u32[]{:S(2)}) collective-permute-start(f32[4,16,1,1024]{3,1,2,0:T(8,128)S(1)} %get-tuple-element.44), channel_id=1, source_target_pairs={{8,0},{16,8},{24,16},{32,24},{40,32},{48,40},{56,48},{64,56},{72,6... | collective-permute-start | bytes 786440 | tf_op jit(solution)/shard_map/ppermute | solution.py:22
  14.8 1.7 fusion.65
  16.5 0.0 copy-done.2
  16.5 0.0 copy-done.3
  16.5 0.6 fusion.66
  17.7 0.9 multiply_add_fusion.3
  18.6 0.2 fusion.64
  18.8 0.1 collective-permute-done.1
  18.9 0.0 collective-permute-done
  19.0 4.2 %broadcast_multiply_fusion = (f32[4,16,16,1024]{3,1,2,0:T(8,128)S(1)}, f32[4,16,16,1024]{3,1,2,0:T(8,128)}) fusion(f32[4,16,16,1]{3,1,2,0:T(8,128)S(1)} %get-tuple-element.47, f32[4,16,16,1023]{3,1,2,0:T(8,128)S(1)} %get-tuple-element.49, f32[4,16,16,1023]{3,1,2,0:T(8,128)S(1)} %get-tuple-element.48, f32[4,16,16,1]{3,1,2,0:T(8,128)S(1)} %get-tuple-element.46, ...), kind=kLoop, calls=%fused_computation.37 | loop fusion | flops 13631488 | bytes 25690112 | tf_op jit(solution)/shard_map/mul | solution.py:87
  23.2 2.1 %multiply_add_fusion.2 = (f32[1,16,16,1024]{3,1,2,0:T(8,128)S(1)}, f32[1,16,16,1024]{3,1,2,0:T(8,128)S(1)}, f32[1,16,16,1024]{3,1,2,0:T(8,128)}, f32[1,16,16,1024]{3,1,2,0:T(8,128)}) fusion(f32[4,16,16,1024]{3,1,2,0:T(8,128)S(1)} %get-tuple-element.7, f32[16,1024]{1,0:T(8,128)S(1)} %get-tuple-element.54, f32[16,1024]{1,0:T(8,128)S(1)} %get-tuple-element.55, ...), kind=kLoop, calls=%fused_computation.52 | loop fusion | flops 5242880 | bytes 8585216 | tf_op jit(solution)/shard_map/add | solution.py:34
  25.3 0.0 copy-start.1
  25.3 3.4 %fusion.60 = (f32[4,16,16,1023]{3,1,2,0:T(8,128)S(1)}, f32[4,16,16,1023]{3,1,2,0:T(8,128)}) fusion(f32[4,16,16,1024]{3,1,2,0:T(8,128)S(1)} %get-tuple-element.7), kind=kLoop, calls=%fused_computation.125 | loop fusion | bytes 16760832 | tf_op jit(solution)/shard_map/jit(_roll_static)/slice | solution.py:85
  28.7 1.1 collective-permute-start.3
  29.8 2.7 %collective-permute-start.2 = (f32[4,16,1,1024]{3,1,2,0:T(8,128)S(1)}, f32[4,16,1,1024]{3,1,2,0:T(8,128)S(1)}, u32[]{:S(2)}, u32[]{:S(2)}) collective-permute-start(f32[4,16,1,1024]{3,1,2,0:T(8,128)S(1)} %get-tuple-element.42), channel_id=1, source_target_pairs={{8,0},{16,8},{24,16},{32,24},{40,32},{48,40},{56,48},{64,56},{72,6... | collective-permute-start | bytes 786440 | tf_op jit(solution)/shard_map/ppermute | solution.py:22
  32.6 0.2 fusion.61
  32.8 5.3 %collective-permute-done.3 = f32[4,16,1,1024]{3,1,2,0:T(8,128)S(1)} collective-permute-done((f32[4,16,1,1024]{3,1,2,0:T(8,128)S(1)}, f32[4,16,1,1024]{3,1,2,0:T(8,128)S(1)}, u32[]{:S(2)}, u32[]{:S(2)}) %collective-permute-start.3) | collective-permute-done | bytes 262176 | tf_op jit(solution)/shard_map/ppermute | solution.py:19
  38.1 0.0 collective-permute-done.2
  38.1 0.0 copy-done.1
  38.1 5.5 %fusion.19 = f32[4,16,16,1024]{3,1,2,0:T(8,128)S(1)} fusion(f32[4,16,16,1024]{3,1,2,0:T(8,128)S(1)} %get-tuple-element.7, f32[4,16,1,1024]{3,1,2,0:T(8,128)S(1)} %collective-permute-done.3, f32[4,16,1,1024]{3,1,2,0:T(8,128)S(1)} %collective-permute-done.2, f32[1,16,16,1024]{3,1,2,0:T(8,128)} %get-tuple-element.21, f32[1,16,16,1024]{3,1,2,0:T(8,128)} %get-tuple-element.20, ...), kind=kLoop, calls=%fused_computation.24 | loop fusion | flops 15728640 | bytes 23592960 | tf_op jit(solution)/shard_map/sub | solution.py:100
  43.6 0.7 multiply_add_fusion.1
  44.4 0.0 copy-start
  44.4 4.7 %fusion.57 = (f32[4,16,16,1023]{3,1,2,0:T(8,128)}, f32[4,16,16,1023]{3,1,2,0:T(8,128)}) fusion(f32[4,16,16,1024]{3,1,2,0:T(8,128)S(1)} %fusion.19), kind=kLoop, calls=%fused_computation.122 | loop fusion | bytes 16760832 | tf_op jit(solution)/shard_map/jit(_roll_static)/slice | solution.py:85
  49.0 0.1 collective-permute-start.5
  49.1 3.7 %collective-permute-start.4 = (f32[4,16,1,1024]{3,1,2,0:T(8,128)S(1)}, f32[4,16,1,1024]{3,1,2,0:T(8,128)S(1)}, u32[]{:S(2)}, u32[]{:S(2)}) collective-permute-start(f32[4,16,1,1024]{3,1,2,0:T(8,128)S(1)} %get-tuple-element.36), channel_id=1, source_target_pairs={{8,0},{16,8},{24,16},{32,24},{40,32},{48,40},{56,48},{64,56},{72,6... | collective-permute-start | bytes 786440 | tf_op jit(solution)/shard_map/ppermute | solution.py:22
  52.9 0.2 fusion.58
  53.1 6.2 %collective-permute-done.5 = f32[4,16,1,1024]{3,1,2,0:T(8,128)S(1)} collective-permute-done((f32[4,16,1,1024]{3,1,2,0:T(8,128)S(1)}, f32[4,16,1,1024]{3,1,2,0:T(8,128)S(1)}, u32[]{:S(2)}, u32[]{:S(2)}) %collective-permute-start.5) | collective-permute-done | bytes 262176 | tf_op jit(solution)/shard_map/ppermute | solution.py:19
  59.3 0.0 collective-permute-done.4
  59.3 0.0 copy-done
  59.3 5.4 %fusion.13 = f32[4,16,16,1024]{3,1,2,0:T(8,128)S(1)} fusion(f32[4,16,16,1024]{3,1,2,0:T(8,128)S(1)} %fusion.19, f32[4,16,1,1024]{3,1,2,0:T(8,128)S(1)} %collective-permute-done.5, f32[4,16,1,1024]{3,1,2,0:T(8,128)S(1)} %collective-permute-done.4, f32[1,16,16,1024]{3,1,2,0:T(8,128)S(1)} %get-tuple-element.17, f32[1,16,16,1024]{3,1,2,0:T(8,128)S(1)} %get-tuple-element.16, ...), kind=kLoop, calls=%fused_computation.16 | loop fusion | flops 15728640 | bytes 25690112 | tf_op jit(solution)/shard_map/sub | solution.py:100
  64.7 2.4 %multiply_add_fusion = (f32[1,16,16,1024]{3,1,2,0:T(8,128)S(1)}, f32[1,16,16,1024]{3,1,2,0:T(8,128)}, f32[1,16,16,1024]{3,1,2,0:T(8,128)}, f32[1,16,16,1024]{3,1,2,0:T(8,128)}) fusion(f32[4,16,16,1024]{3,1,2,0:T(8,128)S(1)} %fusion.13, f32[16,1024]{1,0:T(8,128)S(1)} %get-tuple-element.54, f32[16,1024]{1,0:T(8,128)S(1)} %get-tuple-element.55, ...), kind=kLoop, calls=%fused_computation.44 | loop fusion | flops 5242880 | bytes 8585216 | tf_op jit(solution)/shard_map/add | solution.py:34
  67.1 4.7 %fusion.54 = (f32[4,16,16,1023]{3,1,2,0:T(8,128)}, f32[4,16,16,1023]{3,1,2,0:T(8,128)}) fusion(f32[4,16,16,1024]{3,1,2,0:T(8,128)S(1)} %fusion.13), kind=kLoop, calls=%fused_computation.119 | loop fusion | bytes 16760832 | tf_op jit(solution)/shard_map/jit(_roll_static)/slice | solution.py:85
  71.8 0.0 collective-permute-start.7
  71.8 3.9 %collective-permute-start.6 = (f32[4,16,1,1024]{3,1,2,0:T(8,128)S(1)}, f32[4,16,1,1024]{3,1,2,0:T(8,128)}, u32[]{:S(2)}, u32[]{:S(2)}) collective-permute-start(f32[4,16,1,1024]{3,1,2,0:T(8,128)S(1)} %get-tuple-element.30), channel_id=1, source_target_pairs={{8,0},{16,8},{24,16},{32,24},{40,32},{48,40},{56,48},{64,56},{72,6... | collective-permute-start | bytes 786440 | tf_op jit(solution)/shard_map/ppermute | solution.py:22
  75.6 1.0 fusion.55
  76.7 4.2 %collective-permute-done.7 = f32[4,16,1,1024]{3,1,2,0:T(8,128)S(1)} collective-permute-done((f32[4,16,1,1024]{3,1,2,0:T(8,128)S(1)}, f32[4,16,1,1024]{3,1,2,0:T(8,128)S(1)}, u32[]{:S(2)}, u32[]{:S(2)}) %collective-permute-start.7) | collective-permute-done | bytes 262176 | tf_op jit(solution)/shard_map/ppermute | solution.py:19
  80.8 0.0 collective-permute-done.6
  80.8 12.2 %fusion.7 = f32[4,16,16,1024]{3,1,2,0:T(8,128)} fusion(f32[4,16,16,1024]{3,1,2,0:T(8,128)S(1)} %fusion.19, f32[4,16,16,1024]{3,1,2,0:T(8,128)S(1)} %fusion.13, f32[4,16,1,1024]{3,1,2,0:T(8,128)S(1)} %collective-permute-done.7, f32[4,16,1,1024]{3,1,2,0:T(8,128)} %collective-permute-done.6, f32[1,16,16,1024]{3,1,2,0:T(8,128)} %get-tuple-element.13, ...), kind=kLoop, calls=%fused_computation.8 | loop fusion | flops 25165824 | bytes 31981588 | tf_op jit(solution)/shard_map/add | solution.py:101
  93.1 3.5 %add_reduce_fusion.1 = (f32[16,1024]{1,0:T(8,128)S(1)}, f32[16,1024]{1,0:T(8,128)S(1)}, f32[16,1024]{1,0:T(8,128)S(1)}) fusion(f32[4,16,16,1024]{3,1,2,0:T(8,128)} %fusion.7, f32[4,16,16,1024]{3,1,2,0:T(8,128)S(1)} %copy_convert_fusion), kind=kLoop, calls=%fused_computation.40 | loop fusion | flops 6242304 | bytes 8585216 | tf_op jit(solution)/shard_map/reduce_sum | solution.py:43
  96.6 0.7 maximum_multiply_fusion.4
  97.3 0.0 all-reduce.2.cloned.1.call-update
  97.3 84.9 %all-reduce.2.cloned.1.call-done = f32[3,16,1024]{2,1,0:T(8,128)} async-done(((f32[3,16,1024]{2,1,0:T(8,128)}), f32[3,16,1024]{2,1,0:T(8,128)}) %all-reduce.2.cloned.1.call-update) | async-done | bytes 196624 | tf_op jit(solution)/shard_map/psum | solution.py:105
  182.2 0.9 subtract_bitcast_fusion.2
  183.1 1.0 multiply_reduce_fusion.1
  184.1 0.4 sqrt_cosine_fusion
  184.5 1.7 fusion.25
  186.2 1.6 copy.12
  (5 shorter events, 0.2 us)
Async XLA Ops:
  7.2 175.0 %all-reduce.2.cloned.1.call-start = ((), (), s32[]{:S(2)}) async-start(), calls=%async_computation | async-start | bytes 393216 | tf_op jit(solution)/shard_map/psum | solution.py:105
  10.1 8.9 %collective-permute-start.1 = (f32[4,16,1,1024]{3,1,2,0:T(8,128)S(1)}, f32[4,16,1,1024]{3,1,2,0:T(8,128)S(1)}, u32[]{:S(2)}, u32[]{:S(2)}) collective-permute-start(f32[4,16,1,1024]{3,1,2,0:T(8,128)S(1)} %get-tuple-element.45), channel_id=1, source_target_pairs={{0,8},{8,16},{16,24},{24,32},{32,40},{40,48},{48,56},{56,64},{64,7... | collective-permute-start | bytes 786440 | tf_op jit(solution)/shard_map/ppermute | solution.py:19
  10.2 6.3 %copy-start.2 = (f32[3,16,1024]{2,1,0:T(8,128)S(1)}, f32[3,16,1024]{2,1,0:T(8,128)}, u32[]{:S(2)}) copy-start(f32[3,16,1024]{2,1,0:T(8,128)} %param.5) | copy-start | bytes 589828
  10.2 6.3 %copy-start.3 = (f32[5]{0:T(128)S(1)}, f32[5]{0:T(128)}, u32[]{:S(2)}) copy-start(f32[5]{0:T(128)} %param.6) | copy-start | bytes 64
  10.2 8.7 %collective-permute-start = (f32[4,16,1,1024]{3,1,2,0:T(8,128)S(1)}, f32[4,16,1,1024]{3,1,2,0:T(8,128)S(1)}, u32[]{:S(2)}, u32[]{:S(2)}) collective-permute-start(f32[4,16,1,1024]{3,1,2,0:T(8,128)S(1)} %get-tuple-element.44), channel_id=1, source_target_pairs={{8,0},{16,8},{24,16},{32,24},{40,32},{48,40},{56,48},{64,56},{72,6... | collective-permute-start | bytes 786440 | tf_op jit(solution)/shard_map/ppermute | solution.py:22
  25.3 12.8 %copy-start.1 = (bf16[4,16,16,1024]{3,2,1,0:T(8,128)(2,1)S(1)}, bf16[4,16,16,1024]{3,2,1,0:T(8,128)(2,1)}, u32[]{:S(2)}) copy-start(bf16[4,16,16,1024]{3,2,1,0:T(8,128)(2,1)} %param.4) | copy-start | bytes 6291460
  28.7 9.4 %collective-permute-start.3 = (f32[4,16,1,1024]{3,1,2,0:T(8,128)S(1)}, f32[4,16,1,1024]{3,1,2,0:T(8,128)S(1)}, u32[]{:S(2)}, u32[]{:S(2)}) collective-permute-start(f32[4,16,1,1024]{3,1,2,0:T(8,128)S(1)} %get-tuple-element.43), channel_id=1, source_target_pairs={{0,8},{8,16},{16,24},{24,32},{32,40},{40,48},{48,56},{56,64},{64,7... | collective-permute-start | bytes 786440 | tf_op jit(solution)/shard_map/ppermute | solution.py:19
  29.8 8.3 %collective-permute-start.2 = (f32[4,16,1,1024]{3,1,2,0:T(8,128)S(1)}, f32[4,16,1,1024]{3,1,2,0:T(8,128)S(1)}, u32[]{:S(2)}, u32[]{:S(2)}) collective-permute-start(f32[4,16,1,1024]{3,1,2,0:T(8,128)S(1)} %get-tuple-element.42), channel_id=1, source_target_pairs={{8,0},{16,8},{24,16},{32,24},{40,32},{48,40},{56,48},{64,56},{72,6... | collective-permute-start | bytes 786440 | tf_op jit(solution)/shard_map/ppermute | solution.py:22
  44.4 14.9 %copy-start = (f32[4,16,16,1024]{3,1,2,0:T(8,128)S(1)}, f32[4,16,16,1024]{3,1,2,0:T(8,128)}, u32[]{:S(2)}) copy-start(f32[4,16,16,1024]{3,1,2,0:T(8,128)} %get-tuple-element.8) | copy-start | bytes 12582916
  49.0 10.3 %collective-permute-start.5 = (f32[4,16,1,1024]{3,1,2,0:T(8,128)S(1)}, f32[4,16,1,1024]{3,1,2,0:T(8,128)S(1)}, u32[]{:S(2)}, u32[]{:S(2)}) collective-permute-start(f32[4,16,1,1024]{3,1,2,0:T(8,128)S(1)} %get-tuple-element.37), channel_id=1, source_target_pairs={{0,8},{8,16},{16,24},{24,32},{32,40},{40,48},{48,56},{56,64},{64,7... | collective-permute-start | bytes 786440 | tf_op jit(solution)/shard_map/ppermute | solution.py:19
  49.1 10.1 %collective-permute-start.4 = (f32[4,16,1,1024]{3,1,2,0:T(8,128)S(1)}, f32[4,16,1,1024]{3,1,2,0:T(8,128)S(1)}, u32[]{:S(2)}, u32[]{:S(2)}) collective-permute-start(f32[4,16,1,1024]{3,1,2,0:T(8,128)S(1)} %get-tuple-element.36), channel_id=1, source_target_pairs={{8,0},{16,8},{24,16},{32,24},{40,32},{48,40},{56,48},{64,56},{72,6... | collective-permute-start | bytes 786440 | tf_op jit(solution)/shard_map/ppermute | solution.py:22
  71.8 9.1 %collective-permute-start.7 = (f32[4,16,1,1024]{3,1,2,0:T(8,128)S(1)}, f32[4,16,1,1024]{3,1,2,0:T(8,128)S(1)}, u32[]{:S(2)}, u32[]{:S(2)}) collective-permute-start(f32[4,16,1,1024]{3,1,2,0:T(8,128)S(1)} %get-tuple-element.31), channel_id=1, source_target_pairs={{0,8},{8,16},{16,24},{24,32},{32,40},{40,48},{48,56},{56,64},{64,7... | collective-permute-start | bytes 786440 | tf_op jit(solution)/shard_map/ppermute | solution.py:19
  71.8 9.1 %collective-permute-start.6 = (f32[4,16,1,1024]{3,1,2,0:T(8,128)S(1)}, f32[4,16,1,1024]{3,1,2,0:T(8,128)}, u32[]{:S(2)}, u32[]{:S(2)}) collective-permute-start(f32[4,16,1,1024]{3,1,2,0:T(8,128)S(1)} %get-tuple-element.30), channel_id=1, source_target_pairs={{8,0},{16,8},{24,16},{32,24},{40,32},{48,40},{56,48},{64,56},{72,6... | collective-permute-start | bytes 786440 | tf_op jit(solution)/shard_map/ppermute | solution.py:22
Sparse Core Ops, SparseCore 0:
  97.4 84.7 all-reduce.1
where the time goes:
time: 195 us
  waiting for transfers between devices  101 us (52%)
  other arithmetic  44.4 us (23%)
  local copies, waits for them, and re-layouts  18.4 us (9%)
  starting transfers between devices  16.3 us (8%)
  between operations  14.8 us (8%)
    psum x1, waiting for transfers between devices, shards(): fields = lax.psum(partial_value, 'vec')  84.9 us
    ppermute x4, waiting for transfers between devices, with_halo(): lax.ppermute(lax.slice_in_dim(block, block.shape[dim] - width, None, axis...  15.8 us
    ppermute x4, starting transfers between devices, with_halo(): lax.ppermute(lax.slice_in_dim(block, 0, width, axis=dim), axis, backward)  14.9 us
    slice x6, local copies, waits for them, and re-layouts, apply_hamiltonian(): jnp.roll(middle, -1, 3)  14.1 us
    add x1, other arithmetic, shards(): moments = moments + coefficients[degree + 1] * following  12.2 us
    sub x2, other arithmetic, shards(): following = 2.0 * following - previous  10.8 us
    add x4, other arithmetic, exchange_term(): spin_z * up_real + spin_x * down_real + spin_y * down_imag  6.17 us
    mul x1, other arithmetic, apply_hamiltonian(): inverse_bound * (coupling * exchange_term(middle, spins_here) - hopping *...  4.23 us
  transfers between devices with their start and end apart: 9, of which 5 were waited for; matrix products, arithmetic and copies ran while one was open for 2% of the time, Pallas kernels for 0%

commit v1 on v0

--- a/solution.py
+++ b/solution.py
@@ -102,7 +102,8 @@
         previous = current
         current = following
     partial_value = spin_density(probes, moments) * (coupling / count_all)
-    fields = lax.psum(partial_value, "vec")
+    parts = lax.all_gather(partial_value, "vec")
+    fields = jnp.sum(parts, axis=0)
     rotated = rotate_spins(classical_spins, fields)
     return (rotated, fields)
 

time: 195 us -> 156 us (0.80)
  waiting for transfers between devices: 101 us -> 65.2 us
    psum x1 -> x0, waiting for transfers between devices: 84.9 us -> none  [shards(): fields = lax.psum(partial_value, 'vec')]
    all_gather x0 -> x1, waiting for transfers between devices: none -> 49.4 us  [shards(): parts = lax.all_gather(partial_value, 'vec')]
  transfers between devices with their start and end apart: 9 -> 9, of which waited for: 5 -> 5; matrix products, arithmetic and copies ran while one was open for 2% -> 3% of each run, Pallas kernels for 0% -> 0%
where the time goes in v1:
time: 156 us
  waiting for transfers between devices  65.2 us (42%)
  other arithmetic  43.1 us (28%)
  local copies, waits for them, and re-layouts  16.8 us (11%)
  starting transfers between devices  16.3 us (10%)
  between operations  14.8 us (9%)
    all_gather x1, waiting for transfers between devices, shards(): parts = lax.all_gather(partial_value, 'vec')  49.4 us
    ppermute x4, waiting for transfers between devices, with_halo(): lax.ppermute(lax.slice_in_dim(block, block.shape[dim] - width, None, axis...  15.8 us
    ppermute x4, starting transfers between devices, with_halo(): lax.ppermute(lax.slice_in_dim(block, 0, width, axis=dim), axis, backward)  14.9 us
    slice x6, local copies, waits for them, and re-layouts, apply_hamiltonian(): jnp.roll(middle, -1, 3)  14.1 us
    add x1, other arithmetic, shards(): moments = moments + coefficients[degree + 1] * following  12.2 us
    sub x2, other arithmetic, shards(): following = 2.0 * following - previous  10.8 us
    add x4, other arithmetic, exchange_term(): spin_z * up_real + spin_x * down_real + spin_y * down_imag  6.19 us
    mul x1, other arithmetic, apply_hamiltonian(): inverse_bound * (coupling * exchange_term(middle, spins_here) - hopping *...  4.18 us
  transfers between devices with their start and end apart: 9, of which 5 were waited for; matrix products, arithmetic and copies ran while one was open for 3% of the time, Pallas kernels for 0%

profile of v1, /device:TPU:0, one launch (start us, length us, event | category | flops | bytes accessed | tf_op | source)
XLA Modules:
  0.0 156.2 jit_solution(1615330516895598872)
XLA Ops:
  7.2 0.0 all-gather.2.cloned.1.call-start
  7.2 2.8 %copy_convert_fusion = f32[4,16,16,1024]{3,1,2,0:T(8,128)S(1)} fusion(bf16[4,16,16,1024]{3,2,1,0:T(8,128)(2,1)} %param.4), kind=kLoop, calls=%fused_computation.36 | loop fusion | flops 1048576 | bytes 6291456 | tf_op jit(solution)/shard_map/convert_element_type | solution.py:91
  10.1 0.1 collective-permute-start.1
  10.2 0.0 copy-start.2
  10.2 0.0 copy-start.4
  10.2 4.6 %collective-permute-start = (f32[4,16,1,1024]{3,1,2,0:T(8,128)S(1)}, f32[4,16,1,1024]{3,1,2,0:T(8,128)S(1)}, u32[]{:S(2)}, u32[]{:S(2)}) collective-permute-start(f32[4,16,1,1024]{3,1,2,0:T(8,128)S(1)} %get-tuple-element.44), channel_id=1, source_target_pairs={{8,0},{16,8},{24,16},{32,24},{40,32},{48,40},{56,48},{64,56},{72,6... | collective-permute-start | bytes 786440 | tf_op jit(solution)/shard_map/ppermute | solution.py:22
  14.8 1.7 %fusion.65 = (f32[4,16,16,1023]{3,1,2,0:T(8,128)S(1)}, f32[4,16,16,1023]{3,1,2,0:T(8,128)S(1)}) fusion(f32[4,16,16,1024]{3,1,2,0:T(8,128)S(1)} %copy_convert_fusion), kind=kLoop, calls=%fused_computation.130 | loop fusion | bytes 16760832 | tf_op jit(solution)/shard_map/jit(_roll_static)/slice | solution.py:85
  16.5 0.0 copy-done.2
  16.5 0.0 copy-done.4
  16.5 0.6 fusion.66
  17.8 0.9 multiply_add_fusion.3
  18.7 0.2 fusion.64
  18.9 0.1 collective-permute-done.1
  18.9 0.0 collective-permute-done
  19.0 4.2 %broadcast_multiply_fusion = (f32[4,16,16,1024]{3,1,2,0:T(8,128)S(1)}, f32[4,16,16,1024]{3,1,2,0:T(8,128)}) fusion(f32[4,16,16,1]{3,1,2,0:T(8,128)S(1)} %get-tuple-element.47, f32[4,16,16,1023]{3,1,2,0:T(8,128)S(1)} %get-tuple-element.49, f32[4,16,16,1023]{3,1,2,0:T(8,128)S(1)} %get-tuple-element.48, f32[4,16,16,1]{3,1,2,0:T(8,128)S(1)} %get-tuple-element.46, ...), kind=kLoop, calls=%fused_computation.37 | loop fusion | flops 13631488 | bytes 25690112 | tf_op jit(solution)/shard_map/mul | solution.py:87
  23.2 2.1 %multiply_add_fusion.2 = (f32[1,16,16,1024]{3,1,2,0:T(8,128)S(1)}, f32[1,16,16,1024]{3,1,2,0:T(8,128)S(1)}, f32[1,16,16,1024]{3,1,2,0:T(8,128)}, f32[1,16,16,1024]{3,1,2,0:T(8,128)}) fusion(f32[4,16,16,1024]{3,1,2,0:T(8,128)S(1)} %get-tuple-element.7, f32[16,1024]{1,0:T(8,128)S(1)} %get-tuple-element.54, f32[16,1024]{1,0:T(8,128)S(1)} %get-tuple-element.55, ...), kind=kLoop, calls=%fused_computation.52 | loop fusion | flops 5242880 | bytes 8585216 | tf_op jit(solution)/shard_map/add | solution.py:34
  25.3 0.0 copy-start.1
  25.3 3.4 %fusion.60 = (f32[4,16,16,1023]{3,1,2,0:T(8,128)S(1)}, f32[4,16,16,1023]{3,1,2,0:T(8,128)}) fusion(f32[4,16,16,1024]{3,1,2,0:T(8,128)S(1)} %get-tuple-element.7), kind=kLoop, calls=%fused_computation.125 | loop fusion | bytes 16760832 | tf_op jit(solution)/shard_map/jit(_roll_static)/slice | solution.py:85
  28.7 1.1 collective-permute-start.3
  29.8 2.7 %collective-permute-start.2 = (f32[4,16,1,1024]{3,1,2,0:T(8,128)S(1)}, f32[4,16,1,1024]{3,1,2,0:T(8,128)S(1)}, u32[]{:S(2)}, u32[]{:S(2)}) collective-permute-start(f32[4,16,1,1024]{3,1,2,0:T(8,128)S(1)} %get-tuple-element.42), channel_id=1, source_target_pairs={{8,0},{16,8},{24,16},{32,24},{40,32},{48,40},{56,48},{64,56},{72,6... | collective-permute-start | bytes 786440 | tf_op jit(solution)/shard_map/ppermute | solution.py:22
  32.6 0.2 fusion.61
  32.8 5.3 %collective-permute-done.3 = f32[4,16,1,1024]{3,1,2,0:T(8,128)S(1)} collective-permute-done((f32[4,16,1,1024]{3,1,2,0:T(8,128)S(1)}, f32[4,16,1,1024]{3,1,2,0:T(8,128)S(1)}, u32[]{:S(2)}, u32[]{:S(2)}) %collective-permute-start.3) | collective-permute-done | bytes 262176 | tf_op jit(solution)/shard_map/ppermute | solution.py:19
  38.1 0.0 collective-permute-done.2
  38.1 0.0 copy-done.1
  38.1 5.5 %fusion.19 = f32[4,16,16,1024]{3,1,2,0:T(8,128)S(1)} fusion(f32[4,16,16,1024]{3,1,2,0:T(8,128)S(1)} %get-tuple-element.7, f32[4,16,1,1024]{3,1,2,0:T(8,128)S(1)} %collective-permute-done.3, f32[4,16,1,1024]{3,1,2,0:T(8,128)S(1)} %collective-permute-done.2, f32[1,16,16,1024]{3,1,2,0:T(8,128)} %get-tuple-element.21, f32[1,16,16,1024]{3,1,2,0:T(8,128)} %get-tuple-element.20, ...), kind=kLoop, calls=%fused_computation.24 | loop fusion | flops 15728640 | bytes 23592960 | tf_op jit(solution)/shard_map/sub | solution.py:100
  43.6 0.7 multiply_add_fusion.1
  44.3 0.0 copy-start
  44.3 4.7 %fusion.57 = (f32[4,16,16,1023]{3,1,2,0:T(8,128)}, f32[4,16,16,1023]{3,1,2,0:T(8,128)}) fusion(f32[4,16,16,1024]{3,1,2,0:T(8,128)S(1)} %fusion.19), kind=kLoop, calls=%fused_computation.122 | loop fusion | bytes 16760832 | tf_op jit(solution)/shard_map/jit(_roll_static)/slice | solution.py:85
  49.0 0.1 collective-permute-start.5
  49.1 3.7 %collective-permute-start.4 = (f32[4,16,1,1024]{3,1,2,0:T(8,128)S(1)}, f32[4,16,1,1024]{3,1,2,0:T(8,128)S(1)}, u32[]{:S(2)}, u32[]{:S(2)}) collective-permute-start(f32[4,16,1,1024]{3,1,2,0:T(8,128)S(1)} %get-tuple-element.36), channel_id=1, source_target_pairs={{8,0},{16,8},{24,16},{32,24},{40,32},{48,40},{56,48},{64,56},{72,6... | collective-permute-start | bytes 786440 | tf_op jit(solution)/shard_map/ppermute | solution.py:22
  52.8 0.2 fusion.58
  53.0 6.2 %collective-permute-done.5 = f32[4,16,1,1024]{3,1,2,0:T(8,128)S(1)} collective-permute-done((f32[4,16,1,1024]{3,1,2,0:T(8,128)S(1)}, f32[4,16,1,1024]{3,1,2,0:T(8,128)S(1)}, u32[]{:S(2)}, u32[]{:S(2)}) %collective-permute-start.5) | collective-permute-done | bytes 262176 | tf_op jit(solution)/shard_map/ppermute | solution.py:19
  59.2 0.0 collective-permute-done.4
  59.2 0.0 copy-done
  59.2 5.4 %fusion.13 = f32[4,16,16,1024]{3,1,2,0:T(8,128)S(1)} fusion(f32[4,16,16,1024]{3,1,2,0:T(8,128)S(1)} %fusion.19, f32[4,16,1,1024]{3,1,2,0:T(8,128)S(1)} %collective-permute-done.5, f32[4,16,1,1024]{3,1,2,0:T(8,128)S(1)} %collective-permute-done.4, f32[1,16,16,1024]{3,1,2,0:T(8,128)S(1)} %get-tuple-element.17, f32[1,16,16,1024]{3,1,2,0:T(8,128)S(1)} %get-tuple-element.16, ...), kind=kLoop, calls=%fused_computation.16 | loop fusion | flops 15728640 | bytes 25690112 | tf_op jit(solution)/shard_map/sub | solution.py:100
  64.7 2.4 %multiply_add_fusion = (f32[1,16,16,1024]{3,1,2,0:T(8,128)S(1)}, f32[1,16,16,1024]{3,1,2,0:T(8,128)}, f32[1,16,16,1024]{3,1,2,0:T(8,128)}, f32[1,16,16,1024]{3,1,2,0:T(8,128)}) fusion(f32[4,16,16,1024]{3,1,2,0:T(8,128)S(1)} %fusion.13, f32[16,1024]{1,0:T(8,128)S(1)} %get-tuple-element.54, f32[16,1024]{1,0:T(8,128)S(1)} %get-tuple-element.55, ...), kind=kLoop, calls=%fused_computation.44 | loop fusion | flops 5242880 | bytes 8585216 | tf_op jit(solution)/shard_map/add | solution.py:34
  67.1 4.6 %fusion.54 = (f32[4,16,16,1023]{3,1,2,0:T(8,128)}, f32[4,16,16,1023]{3,1,2,0:T(8,128)}) fusion(f32[4,16,16,1024]{3,1,2,0:T(8,128)S(1)} %fusion.13), kind=kLoop, calls=%fused_computation.119 | loop fusion | bytes 16760832 | tf_op jit(solution)/shard_map/jit(_roll_static)/slice | solution.py:85
  71.8 0.0 collective-permute-start.7
  71.8 3.9 %collective-permute-start.6 = (f32[4,16,1,1024]{3,1,2,0:T(8,128)S(1)}, f32[4,16,1,1024]{3,1,2,0:T(8,128)}, u32[]{:S(2)}, u32[]{:S(2)}) collective-permute-start(f32[4,16,1,1024]{3,1,2,0:T(8,128)S(1)} %get-tuple-element.30), channel_id=1, source_target_pairs={{8,0},{16,8},{24,16},{32,24},{40,32},{48,40},{56,48},{64,56},{72,6... | collective-permute-start | bytes 786440 | tf_op jit(solution)/shard_map/ppermute | solution.py:22
  75.6 1.0 fusion.55
  76.6 4.2 %collective-permute-done.7 = f32[4,16,1,1024]{3,1,2,0:T(8,128)S(1)} collective-permute-done((f32[4,16,1,1024]{3,1,2,0:T(8,128)S(1)}, f32[4,16,1,1024]{3,1,2,0:T(8,128)S(1)}, u32[]{:S(2)}, u32[]{:S(2)}) %collective-permute-start.7) | collective-permute-done | bytes 262176 | tf_op jit(solution)/shard_map/ppermute | solution.py:19
  80.8 0.0 collective-permute-done.6
  80.8 12.2 %fusion.7 = f32[4,16,16,1024]{3,1,2,0:T(8,128)} fusion(f32[4,16,16,1024]{3,1,2,0:T(8,128)S(1)} %fusion.19, f32[4,16,16,1024]{3,1,2,0:T(8,128)S(1)} %fusion.13, f32[4,16,1,1024]{3,1,2,0:T(8,128)S(1)} %collective-permute-done.7, f32[4,16,1,1024]{3,1,2,0:T(8,128)} %collective-permute-done.6, f32[1,16,16,1024]{3,1,2,0:T(8,128)} %get-tuple-element.13, ...), kind=kLoop, calls=%fused_computation.8 | loop fusion | flops 25165824 | bytes 31981588 | tf_op jit(solution)/shard_map/add | solution.py:101
  93.0 3.5 %add_reduce_fusion.1 = (f32[16,1024]{1,0:T(8,128)S(1)}, f32[16,1024]{1,0:T(8,128)S(1)}, f32[16,1024]{1,0:T(8,128)S(1)}) fusion(f32[4,16,16,1024]{3,1,2,0:T(8,128)} %fusion.7, f32[4,16,16,1024]{3,1,2,0:T(8,128)S(1)} %copy_convert_fusion), kind=kLoop, calls=%fused_computation.40 | loop fusion | flops 6242304 | bytes 8585216 | tf_op jit(solution)/shard_map/reduce_sum | solution.py:43
  96.5 0.7 maximum_multiply_fusion.4
  97.2 0.0 all-gather.2.cloned.1.call-update
  97.2 49.4 %all-gather.2.cloned.1.call-done = f32[8,3,16,1024]{3,2,1,0:T(8,128)} async-done(((f32[1,3,16,1024]{3,2,1,0:T(8,128)}), f32[8,3,16,1024]{3,2,1,0:T(8,128)}) %all-gather.2.cloned.1.call-update) | async-done | bytes 1572880 | tf_op jit(solution)/shard_map/all_gather | solution.py:105
  146.6 1.5 reduce_sum.57
  148.1 0.0 copy-start.3
  148.2 0.4 sqrt_cosine_fusion
  148.6 0.7 fusion.25
  149.3 0.0 copy-done.3
  (7 shorter events, 0.2 us)
Async XLA Ops:
  7.2 139.4 %all-gather.2.cloned.1.call-start = ((), (), s32[]{:S(2)}) async-start(), calls=%async_computation | async-start | bytes 1769472 | tf_op jit(solution)/shard_map/all_gather | solution.py:105
  10.1 8.9 %collective-permute-start.1 = (f32[4,16,1,1024]{3,1,2,0:T(8,128)S(1)}, f32[4,16,1,1024]{3,1,2,0:T(8,128)S(1)}, u32[]{:S(2)}, u32[]{:S(2)}) collective-permute-start(f32[4,16,1,1024]{3,1,2,0:T(8,128)S(1)} %get-tuple-element.45), channel_id=1, source_target_pairs={{0,8},{8,16},{16,24},{24,32},{32,40},{40,48},{48,56},{56,64},{64,7... | collective-permute-start | bytes 786440 | tf_op jit(solution)/shard_map/ppermute | solution.py:19
  10.2 6.3 %copy-start.2 = (f32[3,16,1024]{2,1,0:T(8,128)S(1)}, f32[3,16,1024]{2,1,0:T(8,128)}, u32[]{:S(2)}) copy-start(f32[3,16,1024]{2,1,0:T(8,128)} %param.5) | copy-start | bytes 589828
  10.2 6.3 %copy-start.4 = (f32[5]{0:T(128)S(1)}, f32[5]{0:T(128)}, u32[]{:S(2)}) copy-start(f32[5]{0:T(128)} %param.6) | copy-start | bytes 64
  10.2 8.7 %collective-permute-start = (f32[4,16,1,1024]{3,1,2,0:T(8,128)S(1)}, f32[4,16,1,1024]{3,1,2,0:T(8,128)S(1)}, u32[]{:S(2)}, u32[]{:S(2)}) collective-permute-start(f32[4,16,1,1024]{3,1,2,0:T(8,128)S(1)} %get-tuple-element.44), channel_id=1, source_target_pairs={{8,0},{16,8},{24,16},{32,24},{40,32},{48,40},{56,48},{64,56},{72,6... | collective-permute-start | bytes 786440 | tf_op jit(solution)/shard_map/ppermute | solution.py:22
  25.3 12.8 %copy-start.1 = (bf16[4,16,16,1024]{3,2,1,0:T(8,128)(2,1)S(1)}, bf16[4,16,16,1024]{3,2,1,0:T(8,128)(2,1)}, u32[]{:S(2)}) copy-start(bf16[4,16,16,1024]{3,2,1,0:T(8,128)(2,1)} %param.4) | copy-start | bytes 6291460
  28.7 9.4 %collective-permute-start.3 = (f32[4,16,1,1024]{3,1,2,0:T(8,128)S(1)}, f32[4,16,1,1024]{3,1,2,0:T(8,128)S(1)}, u32[]{:S(2)}, u32[]{:S(2)}) collective-permute-start(f32[4,16,1,1024]{3,1,2,0:T(8,128)S(1)} %get-tuple-element.43), channel_id=1, source_target_pairs={{0,8},{8,16},{16,24},{24,32},{32,40},{40,48},{48,56},{56,64},{64,7... | collective-permute-start | bytes 786440 | tf_op jit(solution)/shard_map/ppermute | solution.py:19
  29.8 8.3 %collective-permute-start.2 = (f32[4,16,1,1024]{3,1,2,0:T(8,128)S(1)}, f32[4,16,1,1024]{3,1,2,0:T(8,128)S(1)}, u32[]{:S(2)}, u32[]{:S(2)}) collective-permute-start(f32[4,16,1,1024]{3,1,2,0:T(8,128)S(1)} %get-tuple-element.42), channel_id=1, source_target_pairs={{8,0},{16,8},{24,16},{32,24},{40,32},{48,40},{56,48},{64,56},{72,6... | collective-permute-start | bytes 786440 | tf_op jit(solution)/shard_map/ppermute | solution.py:22
  44.3 14.9 %copy-start = (f32[4,16,16,1024]{3,1,2,0:T(8,128)S(1)}, f32[4,16,16,1024]{3,1,2,0:T(8,128)}, u32[]{:S(2)}) copy-start(f32[4,16,16,1024]{3,1,2,0:T(8,128)} %get-tuple-element.8) | copy-start | bytes 12582916
  49.0 10.3 %collective-permute-start.5 = (f32[4,16,1,1024]{3,1,2,0:T(8,128)S(1)}, f32[4,16,1,1024]{3,1,2,0:T(8,128)S(1)}, u32[]{:S(2)}, u32[]{:S(2)}) collective-permute-start(f32[4,16,1,1024]{3,1,2,0:T(8,128)S(1)} %get-tuple-element.37), channel_id=1, source_target_pairs={{0,8},{8,16},{16,24},{24,32},{32,40},{40,48},{48,56},{56,64},{64,7... | collective-permute-start | bytes 786440 | tf_op jit(solution)/shard_map/ppermute | solution.py:19
  49.1 10.1 %collective-permute-start.4 = (f32[4,16,1,1024]{3,1,2,0:T(8,128)S(1)}, f32[4,16,1,1024]{3,1,2,0:T(8,128)S(1)}, u32[]{:S(2)}, u32[]{:S(2)}) collective-permute-start(f32[4,16,1,1024]{3,1,2,0:T(8,128)S(1)} %get-tuple-element.36), channel_id=1, source_target_pairs={{8,0},{16,8},{24,16},{32,24},{40,32},{48,40},{56,48},{64,56},{72,6... | collective-permute-start | bytes 786440 | tf_op jit(solution)/shard_map/ppermute | solution.py:22
  71.8 9.1 %collective-permute-start.7 = (f32[4,16,1,1024]{3,1,2,0:T(8,128)S(1)}, f32[4,16,1,1024]{3,1,2,0:T(8,128)S(1)}, u32[]{:S(2)}, u32[]{:S(2)}) collective-permute-start(f32[4,16,1,1024]{3,1,2,0:T(8,128)S(1)} %get-tuple-element.31), channel_id=1, source_target_pairs={{0,8},{8,16},{16,24},{24,32},{32,40},{40,48},{48,56},{56,64},{64,7... | collective-permute-start | bytes 786440 | tf_op jit(solution)/shard_map/ppermute | solution.py:19
  71.8 9.1 %collective-permute-start.6 = (f32[4,16,1,1024]{3,1,2,0:T(8,128)S(1)}, f32[4,16,1,1024]{3,1,2,0:T(8,128)}, u32[]{:S(2)}, u32[]{:S(2)}) collective-permute-start(f32[4,16,1,1024]{3,1,2,0:T(8,128)S(1)} %get-tuple-element.30), channel_id=1, source_target_pairs={{8,0},{16,8},{24,16},{32,24},{40,32},{48,40},{56,48},{64,56},{72,6... | collective-permute-start | bytes 786440 | tf_op jit(solution)/shard_map/ppermute | solution.py:22
  148.1 1.2 copy-start.3
Sparse Core Ops, SparseCore 0:
  97.3 49.2 all-gather.1
